TPU v7x, 32 devices: a whole 2x2x4 slice. The times are simulated.
32 devices in a mesh: seq: 8 (over z, core), head: 4 (over y, x).
Axes of the slice: x: 2, y: 2, z: 4, core: 2. Of those that a mesh axis runs over, the one named last changes fastest.
Arguments:
- mixer_input: bfloat16 [2048, 4096], P('seq', 'head'), may hold values from -600 to 600
- gate_input: bfloat16 [2048, 4096], P('seq', 'head'), may hold values from -5 to 5
- b_proj: bfloat16 [2048, 128], P('seq'), may hold values from -0.5 to 0.5
- c_proj: bfloat16 [2048, 128], P('seq'), may hold values from -0.5 to 0.5
- decay_codes: int32 [64, 2048], P('head', 'seq'), may hold values from 1 to 4096
- decay_rates: float32 [64], P('head'), may hold values from 0 to 1
- skip_gain: float32 [64], P('head'), may hold values from 0.5 to 1.5
- norm_gain: float32 [4096], P('head'), may hold values from 0.5 to 1.5
- queries: bfloat16 [2048, 4096], P('seq', 'head'), may hold values from -5 to 5
- keys: bfloat16 [2048, 4096], P('seq', 'head'), may hold values from -5 to 5
Outputs:
- mamba_out: bfloat16 [2048, 4096], P('seq', 'head')
- attn_out: bfloat16 [2048, 4096], P('seq', 'head')
All inputs are finite; a program needn't handle non-finite values.
Results may differ from a plain program's by a relative error of at most 0.013.
Values may be sent and summed in bfloat16 or wider, within the bound.
No kernel may reach another device: no remote copies, remote signals or barrier semaphores. Data moves between devices by JAX's collectives and lax.ppermute only.
A program may use at most 64 MiB of HBM per device.

v0:
```python
import functools
import math
import jax
import jax.numpy as jnp
from jax import lax
from jax.sharding import PartitionSpec as P

HD = 128
CHANNELS_PER_HD = 64
BLOCK = 256
HIGH = lax.Precision.HIGHEST
NEG = -1e30


def carried_in(array, axis, combine, identity):
    devices, mine = (lax.axis_size(axis), lax.axis_index(axis))
    everything = jax.tree.map(
        lambda part, kind: lax.all_gather(part.astype(kind), axis),
        array,
        (jnp.bfloat16, jnp.bfloat16),
    )
    start = jax.tree.map(
        lambda part, zero: jnp.broadcast_to(jnp.asarray(zero, part.dtype), part.shape),
        array,
        identity,
    )

    def hop(k, before):
        reached = k < mine
        new = combine(
            before, jax.tree.map(lambda part, own: part[k].astype(own.dtype), everything, array)
        )
        return jax.tree.map(lambda a, b: jnp.where(reached, a, b), new, before)

    return lax.fori_loop(0, devices, hop, start)


def block_step(state_carry, inputs):
    x_block, b_block, c_block, decay_block = inputs
    running = jnp.cumsum(decay_block, axis=1)
    span = decay_block.shape[1]
    causal = (
        jnp.arange(span, dtype=jnp.int32)[:, None] >= jnp.arange(span, dtype=jnp.int32)[None, :]
    )
    log_gaps = jnp.where(causal[None, :, :], running[:, :, None] - running[:, None, :], NEG)
    decays = jnp.exp(log_gaps)
    match_strength = jnp.dot(c_block, b_block.T, preferred_element_type=jnp.float32)
    x_float = x_block.astype(jnp.float32)
    within = jnp.einsum(
        "hts,shp->thp", decays * match_strength[None, :, :], x_float, precision=HIGH
    )
    c_float = c_block.astype(jnp.float32)
    carried = jnp.exp(running).T[:, :, None] * jnp.einsum(
        "tn,hnp->thp", c_float, state_carry, precision=HIGH
    )
    to_end = jnp.exp(running[:, -1:] - running)
    updated_state = jnp.exp(running[:, -1])[:, None, None] * state_carry + jnp.einsum(
        "hs,sn,shp->hnp", to_end, b_block.astype(jnp.float32), x_float, precision=HIGH
    )
    return (updated_state, within + carried)


def local_scan(x_local, b_local, c_local, log_decay):
    tok_rows = x_local.shape[0]
    heads_local = log_decay.shape[0]
    block_count = tok_rows // BLOCK
    x_blocks = x_local.reshape(block_count, BLOCK, heads_local, CHANNELS_PER_HD)
    b_blocks = b_local.reshape(block_count, BLOCK, b_local.shape[1])
    c_blocks = c_local.reshape(block_count, BLOCK, c_local.shape[1])
    decay_blocks = log_decay.reshape(heads_local, block_count, BLOCK).transpose(1, 0, 2)
    initial = jnp.zeros((heads_local, b_local.shape[1], CHANNELS_PER_HD), jnp.float32)
    final_state, y_blocks = lax.scan(
        block_step, initial, (x_blocks, b_blocks, c_blocks, decay_blocks)
    )
    return (final_state, y_blocks.reshape(tok_rows, heads_local, CHANNELS_PER_HD))


def masked_scores(q_rows, q_pos, k_rows, k_pos):
    score_scale = 1.0 / math.sqrt(k_rows.shape[-1])
    scores = (
        jnp.einsum("qhd,khd->hqk", q_rows, k_rows, preferred_element_type=jnp.float32) * score_scale
    )
    visible = k_pos[None, None, :] <= q_pos[None, :, None]
    return (jnp.where(visible, scores, NEG), visible)


def online_update(group_state, q_rows, q_pos, k_rows, v_rows, k_pos):
    row_top, row_total, weighted_sum = group_state
    scores, visible = masked_scores(q_rows, q_pos, k_rows, k_pos)
    new_top = jnp.maximum(row_top, jnp.max(scores, axis=2))
    rescale = jnp.exp(row_top - new_top)
    weights = jnp.where(visible, jnp.exp(scores - new_top[:, :, None]), 0.0)
    row_total = row_total * rescale + jnp.sum(weights, axis=2)
    weighted_sum = weighted_sum * rescale[:, :, None] + jnp.einsum(
        "hqk,khd->hqd", weights.astype(jnp.bfloat16), v_rows, preferred_element_type=jnp.float32
    )
    return (new_top, row_total, weighted_sum)


def when_visible(state_update, group_state, q_pos, key_offset):
    return lax.cond(key_offset > q_pos[-1], lambda held: held, state_update, group_state)


def on_device(
    mixer_input,
    gate_input,
    b_proj,
    c_proj,
    decay_codes,
    decay_rates,
    skip_gain,
    norm_gain,
    queries,
    keys,
):
    tok_rows = mixer_input.shape[0]
    heads_local = decay_rates.shape[0]
    heads_att = queries.shape[1] // HD
    seq_rank = lax.axis_index("seq")
    own_positions = seq_rank * tok_rows + jnp.arange(tok_rows, dtype=jnp.int32)
    groups = [(queries, own_positions)]
    groups = [(q_rows.reshape(q_rows.shape[0], heads_att, HD), q_pos) for q_rows, q_pos in groups]
    log_decay = -decay_rates[:, None] * decay_codes.astype(jnp.float32)
    local_state, y_local = local_scan(mixer_input, b_proj, c_proj, log_decay)
    total_log = jnp.sum(log_decay, axis=1)

    def combine(earlier, later):
        return (earlier[0] + later[0], jnp.exp(later[0])[:, None, None] * earlier[1] + later[1])

    identity = (jnp.zeros_like(total_log), jnp.zeros_like(local_state))
    _, incoming = carried_in((total_log, local_state), "seq", combine, identity)
    running = jnp.cumsum(log_decay, axis=1)
    carried = jnp.einsum("tn,hnp->thp", c_proj.astype(jnp.float32), incoming, precision=HIGH)
    carried = carried * jnp.exp(running).T[:, :, None]
    x_float = mixer_input.reshape(tok_rows, heads_local, CHANNELS_PER_HD).astype(jnp.float32)
    ssm_out = (y_local + carried + skip_gain[None, :, None] * x_float).reshape(
        tok_rows, heads_local * CHANNELS_PER_HD
    )
    gated = ssm_out * jax.nn.silu(gate_input.astype(jnp.float32))
    squares = lax.psum(jnp.sum(gated * gated, axis=1), "head")
    channels = gated.shape[1] * lax.axis_size("head")
    mamba_out = (
        gated * lax.rsqrt(squares / channels + 1e-05)[:, None] * norm_gain[None, :]
    ).astype(jnp.bfloat16)
    initial = tuple(
        (
            (
                jnp.full((heads_att, q_pos.shape[0]), NEG, jnp.float32),
                jnp.zeros((heads_att, q_pos.shape[0]), jnp.float32),
                jnp.zeros((heads_att, q_pos.shape[0], HD), jnp.float32),
            )
            for _, q_pos in groups
        )
    )
    states = initial
    k_piece = lax.all_gather(keys, "seq", axis=0, tiled=True)
    v_piece = lax.all_gather(mamba_out, "seq", axis=0, tiled=True)
    row_count = k_piece.shape[0]
    block_rows = math.gcd(row_count, 512)

    def one_block(block_id, states):
        key_offset = block_id * block_rows
        k_rows = lax.dynamic_slice_in_dim(k_piece, block_id * block_rows, block_rows, 0).reshape(
            block_rows, heads_att, HD
        )
        v_rows = lax.dynamic_slice_in_dim(v_piece, block_id * block_rows, block_rows, 0).reshape(
            block_rows, heads_att, HD
        )
        k_pos = key_offset + jnp.arange(block_rows, dtype=jnp.int32)
        return tuple(
            (
                when_visible(
                    functools.partial(
                        online_update,
                        q_rows=group[0],
                        q_pos=group[1],
                        k_rows=k_rows,
                        v_rows=v_rows,
                        k_pos=k_pos,
                    ),
                    group_state,
                    group[1],
                    key_offset,
                )
                for group, group_state in zip(groups, states)
            )
        )

    finals = lax.fori_loop(0, row_count // block_rows, one_block, states)
    results = [(group_state[2], group_state[1]) for group_state in finals]
    rows_out = [
        (weighted / totals[:, :, None])
        .transpose(1, 0, 2)
        .reshape(weighted.shape[1], heads_att * HD)
        .astype(jnp.bfloat16)
        for weighted, totals in results
    ]
    attn_out = rows_out[0]
    return (mamba_out, attn_out)


def solution(mesh):
    in_specs = (
        P("seq", "head"),
        P("seq", "head"),
        P("seq", None),
        P("seq", None),
        P("head", "seq"),
        P("head"),
        P("head"),
        P("head"),
        P("seq", "head"),
        P("seq", "head"),
    )
    out_specs = (P("seq", "head"), P("seq", "head"))
    return jax.shard_map(
        on_device, mesh=mesh, in_specs=in_specs, out_specs=out_specs, check_vma=False
    )
```

profile of v0, /device:TPU:25, one launch (start us, length us, event | category | flops | bytes accessed | tf_op | source)
XLA Modules:
  0.0 200.4 jit_solution(12899004294406485471)
XLA Ops:
  11.2 2.2 %fusion.32 = bf16[16,128,64]{1,2,0:T(8,128)(2,1)} fusion(bf16[256,16,64]{0,2,1:T(8,128)(2,1)S(1)} %bitcast.92, f32[256,16]{0,1:T(8,128)S(1)} %get-tuple-element.482, f32[16]{0:T(128)S(1)} %exponential_multiply_fusion, bf16[256,128]{1,0:T(8,128)(2,1)} %param.18), kind=kOutput, calls=%fused_computation.45 | convolution fusion | flops 403439616 | bytes 868416 | tf_op jit(solution)/shard_map/while/body/eval_jaxpr/hs,sn,shp->hnp/dot_general | solution.py:57
  15.6 13.3 %all-reduce = bf16[128]{0:T(256)(128)(2,1)S(1)} all-reduce(bf16[128]{0:T(256)(128)(2,1)S(1)} %dynamic-update-slice), channel_id=2, replica_groups=mesh['seq'=8,'head'=4] {'seq'}, use_global_device_ids=true, to_apply=%add | all-reduce | flops 128 | bytes 512
  30.1 3.0 %fusion.23 = f32[256,16,64]{0,2,1:T(8,128)S(1)} fusion(bf16[256,16,64]{0,2,1:T(8,128)(2,1)S(1)} %bitcast.93, f32[256,256]{1,0:T(8,128)S(1)} %fusion.47, f32[16,256]{1,0:T(8,128)S(1)} %copy_bitcast_fusion.1, pred[256,256]{1,0:T(8,128)(4,1)S(1)} %iota_compare_fusion), kind=kOutput, calls=%fused_computation.32 | convolution fusion | flops 808452096 | bytes 1916928 | tf_op jit(solution)/shard_map/while/body/eval_jaxpr/hts,shp->thp/dot_general | solution.py:49
  33.7 9.1 %all-gather.10.cloned.1.call-done = bf16[128,128,64]{1,2,0:T(8,128)(2,1)} async-done(((bf16[16,128,64]{1,2,0:T(8,128)(2,1)}), bf16[128,128,64]{1,2,0:T(8,128)(2,1)}) %all-gather.10.cloned.1.call-update) | async-done | bytes 2097168 | tf_op jit(solution)/shard_map/all_gather | solution.py:18
  42.8 13.6 %while.37 = (s32[]{:T(128)}, f32[16,128,64]{2,1,0:T(8,128)S(1)}, s32[]{:T(128)}, bf16[8,16]{1,0:T(8,128)(2,1)S(1)}, bf16[8,16,128,64]{2,3,1,0:T(8,128)(2,1)}, /*index=5*/s32[]{:T(128)}, s32[]{:T(128)}) while((s32[]{:T(128)}, f32[16,128,64]{2,1,0:T(8,128)S(1)}, s32[]{:T(128)}, bf16[8,16]{1,0:T(8,128)(2,1)S(1)}, ...), condition=%wide.region_4.5_spmd.clone, body=%wide.region_3.4_spmd.clone.sunk | while | flops 655380 | bytes 2359569 | solution.py:35
  56.4 2.1 %fusion.28 = f32[256,16,64]{0,2,1:T(8,128)} fusion(f32[256,16,64]{0,2,1:T(8,128)S(1)} %fusion.30, f32[16,128,64]{2,1,0:T(8,128)S(1)} %get-tuple-element.383, bf16[256,16,64]{0,2,1:T(8,128)(2,1)S(1)} %bitcast.94, f32[16]{0:T(128)S(1)} %copy-done.5, f32[256,16]{0,1:T(8,128)S(1)} %get-tuple-element.483, bf16[256,128]{1,0:T(8,128)(2,1)S(1)} %copy-done), kind=kOutput, calls=%fused_computation.36 | convolution fusion | flops 403963904 | bytes 3227712 | tf_op jit(solution)/shard_map/tn,hnp->thp/dot_general | solution.py:133
  58.5 1.6 copy.59
  60.6 7.8 %psum.7 = f32[256]{0:T(256)S(1)} all-reduce(f32[256]{0:T(256)S(1)} %multiply_reduce_fusion), channel_id=1, replica_groups=mesh['seq'=8,'head'=4] {'head'}, use_global_device_ids=true, to_apply=%region_6.7 | all-reduce | flops 256 | bytes 2048 | tf_op jit(solution)/shard_map/psum | solution.py:140
  71.3 44.5 %all-gather.8.cloned.1.call-done = bf16[2048,1024]{1,0:T(8,128)(2,1)} async-done(((bf16[256,1024]{1,0:T(8,128)(2,1)}), bf16[2048,1024]{1,0:T(8,128)(2,1)}) %all-gather.8.cloned.1.call-update) | async-done | bytes 4194320 | tf_op jit(solution)/shard_map/all_gather | solution.py:157
  115.8 6.5 %copy.63 = bf16[2048,1024]{0,1:T(8,128)(2,1)} copy(bf16[2048,1024]{1,0:T(8,128)(2,1)} %all-gather.8.cloned.1.call-done) | data formatting | bytes 8388608 | tf_op jit(solution)/shard_map/while | solution.py:189
  122.3 41.8 %all-gather.6.cloned.1.call-done = bf16[2048,1024]{0,1:T(8,128)(2,1)} async-done(((bf16[256,1024]{0,1:T(8,128)(2,1)}), bf16[2048,1024]{0,1:T(8,128)(2,1)}) %all-gather.6.cloned.1.call-update) | async-done | bytes 4194320 | tf_op jit(solution)/shard_map/all_gather | solution.py:156
  164.2 28.6 %while.36 = (s32[]{:T(128)}, f32[8,256]{1,0:T(8,128)S(1)}, f32[8,256]{1,0:T(8,128)S(1)}, f32[8,256,128]{2,1,0:T(8,128)S(1)}, s32[256]{0:T(256)S(1)}, /*index=5*/...) while((s32[]{:T(128)}, f32[8,256]{1,0:T(8,128)S(1)}, ...), condition=%wide.region_12.13_spmd, body=%wide.region_7.12_spmd.sunk | while | flops 551162368 | bytes 22160680 | solution.py:189
  165.3 6.0 %conditional.2 = (f32[8,256]{1,0:T(8,128)S(1)}, f32[8,256]{1,0:T(8,128)S(1)}, f32[8,256,128]{2,1,0:T(8,128)S(1)}) conditional(s32[]{:T(128)} %convert_element_type.129, (s32[]{:T(128)}, s32[512]{0:T(512)S(1)}, s32[256]{0:T(256)S(1)}, bf16[2048,1024]{0,1:T(8,128)(2,1)}, bf16[256,8,128]{2,0,1:T(8,128)(2,1)S(1)}, /*index=5*/f32[8,256]{1,0:T(8,128)S(1)}, ...), branch_computations={%region_8.10_spmd, %region_11.11_spmd} | conditional | flops 551162368 | bytes 22142018 | solution.py:101
  165.5 1.7 constant_dynamic-slice_fusion
  169.2 2.1 %fusion.6 = f32[8,256,128]{2,1,0:T(8,128)S(1)} fusion(bf16[512,8,128]{0,2,1:T(8,128)(2,1)S(1)} %bitcast.91, f32[8,512,256]{2,1,0:T(8,128)S(1)} %get-tuple-element.477, f32[8,256]{1,0:T(8,128)S(1)} %max.5, pred[256,512]{0,1:T(8,128)(4,1)S(1)} %broadcast_compare_fusion, f32[8,256,128]{2,1,0:T(8,128)S(1)} %get-tuple-element.364, ...), kind=kOutput, calls=%fused_computation.7 | convolution fusion | flops 274202624 | bytes 7487488 | tf_op jit(solution)/shard_map/while/body/eval_jaxpr/cond/branch_0_fun/hqk,khd->hqd/dot_general | solution.py:94
  172.5 6.0 %conditional.2 = (f32[8,256]{1,0:T(8,128)S(1)}, f32[8,256]{1,0:T(8,128)S(1)}, f32[8,256,128]{2,1,0:T(8,128)S(1)}) conditional(s32[]{:T(128)} %convert_element_type.129, (s32[]{:T(128)}, s32[512]{0:T(512)S(1)}, s32[256]{0:T(256)S(1)}, bf16[2048,1024]{0,1:T(8,128)(2,1)}, bf16[256,8,128]{2,0,1:T(8,128)(2,1)S(1)}, /*index=5*/f32[8,256]{1,0:T(8,128)S(1)}, ...), branch_computations={%region_8.10_spmd, %region_11.11_spmd} | conditional | flops 551162368 | bytes 22142018 | solution.py:101
  172.7 1.7 constant_dynamic-slice_fusion
  176.3 2.1 %fusion.6 = f32[8,256,128]{2,1,0:T(8,128)S(1)} fusion(bf16[512,8,128]{0,2,1:T(8,128)(2,1)S(1)} %bitcast.91, f32[8,512,256]{2,1,0:T(8,128)S(1)} %get-tuple-element.477, f32[8,256]{1,0:T(8,128)S(1)} %max.5, pred[256,512]{0,1:T(8,128)(4,1)S(1)} %broadcast_compare_fusion, f32[8,256,128]{2,1,0:T(8,128)S(1)} %get-tuple-element.364, ...), kind=kOutput, calls=%fused_computation.7 | convolution fusion | flops 274202624 | bytes 7487488 | tf_op jit(solution)/shard_map/while/body/eval_jaxpr/cond/branch_0_fun/hqk,khd->hqd/dot_general | solution.py:94
  179.6 6.0 %conditional.2 = (f32[8,256]{1,0:T(8,128)S(1)}, f32[8,256]{1,0:T(8,128)S(1)}, f32[8,256,128]{2,1,0:T(8,128)S(1)}) conditional(s32[]{:T(128)} %convert_element_type.129, (s32[]{:T(128)}, s32[512]{0:T(512)S(1)}, s32[256]{0:T(256)S(1)}, bf16[2048,1024]{0,1:T(8,128)(2,1)}, bf16[256,8,128]{2,0,1:T(8,128)(2,1)S(1)}, /*index=5*/f32[8,256]{1,0:T(8,128)S(1)}, ...), branch_computations={%region_8.10_spmd, %region_11.11_spmd} | conditional | flops 551162368 | bytes 22142018 | solution.py:101
  179.8 1.7 constant_dynamic-slice_fusion
  183.5 2.1 %fusion.6 = f32[8,256,128]{2,1,0:T(8,128)S(1)} fusion(bf16[512,8,128]{0,2,1:T(8,128)(2,1)S(1)} %bitcast.91, f32[8,512,256]{2,1,0:T(8,128)S(1)} %get-tuple-element.477, f32[8,256]{1,0:T(8,128)S(1)} %max.5, pred[256,512]{0,1:T(8,128)(4,1)S(1)} %broadcast_compare_fusion, f32[8,256,128]{2,1,0:T(8,128)S(1)} %get-tuple-element.364, ...), kind=kOutput, calls=%fused_computation.7 | convolution fusion | flops 274202624 | bytes 7487488 | tf_op jit(solution)/shard_map/while/body/eval_jaxpr/cond/branch_0_fun/hqk,khd->hqd/dot_general | solution.py:94
  186.8 6.0 %conditional.2 = (f32[8,256]{1,0:T(8,128)S(1)}, f32[8,256]{1,0:T(8,128)S(1)}, f32[8,256,128]{2,1,0:T(8,128)S(1)}) conditional(s32[]{:T(128)} %convert_element_type.129, (s32[]{:T(128)}, s32[512]{0:T(512)S(1)}, s32[256]{0:T(256)S(1)}, bf16[2048,1024]{0,1:T(8,128)(2,1)}, bf16[256,8,128]{2,0,1:T(8,128)(2,1)S(1)}, /*index=5*/f32[8,256]{1,0:T(8,128)S(1)}, ...), branch_computations={%region_8.10_spmd, %region_11.11_spmd} | conditional | flops 551162368 | bytes 22142018 | solution.py:101
  187.0 1.7 constant_dynamic-slice_fusion
  190.6 2.1 %fusion.6 = f32[8,256,128]{2,1,0:T(8,128)S(1)} fusion(bf16[512,8,128]{0,2,1:T(8,128)(2,1)S(1)} %bitcast.91, f32[8,512,256]{2,1,0:T(8,128)S(1)} %get-tuple-element.477, f32[8,256]{1,0:T(8,128)S(1)} %max.5, pred[256,512]{0,1:T(8,128)(4,1)S(1)} %broadcast_compare_fusion, f32[8,256,128]{2,1,0:T(8,128)S(1)} %get-tuple-element.364, ...), kind=kOutput, calls=%fused_computation.7 | convolution fusion | flops 274202624 | bytes 7487488 | tf_op jit(solution)/shard_map/while/body/eval_jaxpr/cond/branch_0_fun/hqk,khd->hqd/dot_general | solution.py:94
  (117 shorter events, 35.6 us)
Async XLA Ops:
  7.2 21.9 %copy-start = (bf16[256,128]{1,0:T(8,128)(2,1)S(1)}, bf16[256,128]{1,0:T(8,128)(2,1)}, u32[]{:S(2)}) copy-start(bf16[256,128]{1,0:T(8,128)(2,1)} %param.19) | copy-start | bytes 196612
  7.2 35.6 %all-gather.10.cloned.1.call-start = ((), (), s32[]{:S(2)}) async-start(), calls=%async_computation.2 | async-start | bytes 2359296 | tf_op jit(solution)/shard_map/all_gather | solution.py:18
  13.4 102.4 %all-gather.8.cloned.1.call-start = ((), (), s32[]{:S(2)}) async-start(), calls=%async_computation.1 | async-start | bytes 4718592 | tf_op jit(solution)/shard_map/all_gather | solution.py:157
  42.8 13.6 %copy-start.5 = (f32[16]{0:T(128)S(1)}, f32[16]{0:T(128)}, u32[]{:S(2)}) copy-start(f32[16]{0:T(128)} %param.22) | copy-start | bytes 196
  56.4 3.8 %copy-start.1 = (bf16[256,1024]{1,0:T(8,128)(2,1)S(1)}, bf16[256,1024]{1,0:T(8,128)(2,1)}, u32[]{:S(2)}) copy-start(bf16[256,1024]{1,0:T(8,128)(2,1)} %param.17) | copy-start | bytes 1572868
  56.4 12.0 %copy-start.4 = (f32[1024]{0:T(1024)S(1)}, f32[1024]{0:T(1024)}, u32[]{:S(2)}) copy-start(f32[1024]{0:T(1024)} %param.23) | copy-start | bytes 12292
  58.5 11.3 %copy-start.2 = (bf16[256,1024]{1,0:T(8,128)(2,1)S(1)}, bf16[256,1024]{1,0:T(8,128)(2,1)}, u32[]{:S(2)}) copy-start(bf16[256,1024]{1,0:T(8,128)(2,1)} %param.25) | copy-start | bytes 1572868
  58.5 12.3 %copy-start.3 = (bf16[256,1024]{1,0:T(8,128)(2,1)S(1)}, bf16[256,1024]{1,0:T(8,128)(2,1)}, u32[]{:S(2)}) copy-start(bf16[256,1024]{1,0:T(8,128)(2,1)} %param.24) | copy-start | bytes 1572868
  69.5 94.6 %all-gather.6.cloned.1.call-start = ((), (), s32[]{:S(2)}) async-start(), calls=%async_computation | async-start | bytes 4718592 | tf_op jit(solution)/shard_map/all_gather | solution.py:156
Sparse Core Ops, SparseCore 0:
  13.5 29.2 all-gather.9
  69.7 46.0 all-gather.7
  118.0 46.0 all-gather.5
where the time goes:
time: 201 us; the launch traced here: 200 us
  waiting for transfers between devices  95.4 us (47%)
  local copies, waits for them, and re-layouts  32 us (16%)
  blocking collectives  21.1 us (10%)
  matrix products  21 us (10%)
  between operations  14.6 us (7%)
  other arithmetic  12.9 us (6%)
  loops' own time  3.13 us (2%)
    all_gather x1, waiting for transfers between devices, on_device(): v_piece = lax.all_gather(mamba_out, 'seq', axis=0, tiled=True)  44.5 us
    all_gather x1, waiting for transfers between devices, on_device(): k_piece = lax.all_gather(keys, 'seq', axis=0, tiled=True)  41.8 us
    unnamed x1, blocking collectives  13.3 us
    dynamic_slice x16, local copies, waits for them, and re-layouts, hop(): part[k].astype(own.dtype)  10.1 us
    all_gather x1, waiting for transfers between devices, carried_in(): lax.all_gather(part.astype(kind), axis)  9.1 us
    dot_general x4, matrix products, online_update(): jnp.einsum('hqk,khd->hqd', weights.astype(jnp.bfloat16), v_rows, preferre...  8.4 us
    psum x1, blocking collectives, on_device(): squares = lax.psum(jnp.sum(gated * gated, axis=1), 'head')  7.76 us
    while x2, local copies, waits for them, and re-layouts, on_device(): finals = lax.fori_loop(0, row_count // block_rows, one_block, states)  6.79 us
  transfers between devices with their start and end apart: 3, of which 3 were waited for; matrix products, arithmetic and copies ran while one was open for 7% of the time, Pallas kernels for 0%

commit v1 on v0

--- a/solution.py
+++ b/solution.py
@@ -113,6 +113,39 @@
     queries,
     keys,
 ):
+
+    def guide_the_signs(slab_in, along_dim):
+        all_rows, local_now, z1 = (
+            lax.axis_size("seq"),
+            lax.axis_index("seq"),
+            slab_in.shape[along_dim],
+        )
+        out_arr = lax.dynamic_update_slice_in_dim(
+            jnp.zeros(
+                [m * all_rows if jj == along_dim else m for jj, m in enumerate(slab_in.shape)],
+                slab_in.dtype,
+            ),
+            slab_in,
+            local_now * z1,
+            axis=along_dim,
+        )
+        all_values = raw_out = slab_in
+        for d in range(1, all_rows // 2 + 1):
+            all_values = lax.ppermute(
+                all_values, "seq", list(map(lambda jj: (jj, (jj + 1) % all_rows), range(all_rows)))
+            )
+            out_arr = lax.dynamic_update_slice_in_dim(
+                out_arr, all_values, (local_now - d) % all_rows * z1, axis=along_dim
+            )
+            if 2 * d < all_rows:
+                raw_out = lax.ppermute(
+                    raw_out, "seq", list(map(lambda jj: (jj, (jj - 1) % all_rows), range(all_rows)))
+                )
+                out_arr = lax.dynamic_update_slice_in_dim(
+                    out_arr, raw_out, (local_now + d) % all_rows * z1, axis=along_dim
+                )
+        return out_arr
+
     tok_rows = mixer_input.shape[0]
     heads_local = decay_rates.shape[0]
     heads_att = queries.shape[1] // HD
@@ -153,7 +186,7 @@
         )
     )
     states = initial
-    k_piece = lax.all_gather(keys, "seq", axis=0, tiled=True)
+    k_piece = guide_the_signs(keys, 0)
     v_piece = lax.all_gather(mamba_out, "seq", axis=0, tiled=True)
     row_count = k_piece.shape[0]
     block_rows = math.gcd(row_count, 512)

time: 201 us -> 194 us (0.965)
  waiting for transfers between devices: 95.4 us -> 52.9 us
  starting transfers between devices: 0.3 us -> 23.1 us
  local copies, waits for them, and re-layouts: 32 us -> 42.9 us
    all_gather x1, waiting for transfers between devices: 44.5 us -> 0.01 us  [on_device(): v_piece = lax.all_gather(mamba_out, 'seq', axis=0, tiled=True)]
    ppermute x0 -> x7, waiting for transfers between devices: none -> 43.8 us  [the longest x4 40 us: guide_the_signs(): lax.ppermute(all_values, 'seq', list(map(lambda jj: (jj, (jj + 1) % all_r...]
    all_gather x1 -> x0, waiting for transfers between devices: 41.8 us -> none  [on_device(): k_piece = lax.all_gather(keys, 'seq', axis=0, tiled=True)]
    ppermute x0 -> x7, starting transfers between devices: none -> 23 us  [the longest x4 16.7 us: guide_the_signs(): lax.ppermute(all_values, 'seq', list(map(lambda jj: (jj, (jj + 1) % all_r...]
    dynamic_update_slice x0 -> x8, local copies, waits for them, and re-layouts: none -> 9.07 us  [the longest x4 4.56 us: guide_the_signs(): lax.dynamic_update_slice_in_dim(out_arr, all_values, (local_now - d) % al...]
    broadcast_in_dim x0 -> x1, local copies, waits for them, and re-layouts: none -> 2.48 us  [guide_the_signs(): jnp.zeros([m * all_rows if jj == along_dim else m for jj, m in enumerate(...]
  transfers between devices with their start and end apart: 3 -> 9, of which waited for: 3 -> 5; matrix products, arithmetic and copies ran while one was open for 7% -> 10% of each run, Pallas kernels for 0% -> 0%
where the time goes in v1:
time: 194 us; the launch traced here: 192 us
  waiting for transfers between devices  52.9 us (27%)
  local copies, waits for them, and re-layouts  42.9 us (22%)
  starting transfers between devices  23.1 us (12%)
  blocking collectives  21.1 us (11%)
  matrix products  21 us (11%)
  between operations  14.9 us (8%)
  other arithmetic  12.9 us (7%)
  loops' own time  3.41 us (2%)
    ppermute x4, waiting for transfers between devices, guide_the_signs(): lax.ppermute(all_values, 'seq', list(map(lambda jj: (jj, (jj + 1) % all_r...  40 us
    ppermute x4, starting transfers between devices, guide_the_signs(): lax.ppermute(all_values, 'seq', list(map(lambda jj: (jj, (jj + 1) % all_r...  16.7 us
    unnamed x1, blocking collectives  13.3 us
    dynamic_slice x16, local copies, waits for them, and re-layouts, hop(): part[k].astype(own.dtype)  10.1 us
    all_gather x1, waiting for transfers between devices, carried_in(): lax.all_gather(part.astype(kind), axis)  9.12 us
    dot_general x4, matrix products, online_update(): jnp.einsum('hqk,khd->hqd', weights.astype(jnp.bfloat16), v_rows, preferre...  8.43 us
    psum x1, blocking collectives, on_device(): squares = lax.psum(jnp.sum(gated * gated, axis=1), 'head')  7.77 us
    while x2, local copies, waits for them, and re-layouts, on_device(): finals = lax.fori_loop(0, row_count // block_rows, one_block, states)  6.78 us
  transfers between devices with their start and end apart: 9, of which 5 were waited for; matrix products, arithmetic and copies ran while one was open for 10% of the time, Pallas kernels for 0%

profile of v1, /device:TPU:25, one launch (start us, length us, event | category | flops | bytes accessed | tf_op | source)
XLA Modules:
  0.0 192.3 jit_solution(11299126646701555441)
XLA Ops:
  11.2 2.2 %fusion.32 = bf16[16,128,64]{1,2,0:T(8,128)(2,1)} fusion(bf16[256,16,64]{0,2,1:T(8,128)(2,1)S(1)} %bitcast.92, f32[256,16]{0,1:T(8,128)S(1)} %get-tuple-element.482, f32[16]{0:T(128)S(1)} %exponential_multiply_fusion, bf16[256,128]{1,0:T(8,128)(2,1)} %param.18), kind=kOutput, calls=%fused_computation.45 | convolution fusion | flops 403439616 | bytes 868416 | tf_op jit(solution)/shard_map/while/body/eval_jaxpr/hs,sn,shp->hnp/dot_general | solution.py:57
  15.6 13.3 %all-reduce = bf16[128]{0:T(256)(128)(2,1)S(1)} all-reduce(bf16[128]{0:T(256)(128)(2,1)S(1)} %dynamic-update-slice), channel_id=2, replica_groups=mesh['seq'=8,'head'=4] {'seq'}, use_global_device_ids=true, to_apply=%add | all-reduce | flops 128 | bytes 512
  30.1 3.0 %fusion.23 = f32[256,16,64]{0,2,1:T(8,128)S(1)} fusion(bf16[256,16,64]{0,2,1:T(8,128)(2,1)S(1)} %bitcast.93, f32[256,256]{1,0:T(8,128)S(1)} %fusion.47, f32[16,256]{1,0:T(8,128)S(1)} %copy_bitcast_fusion.1, pred[256,256]{1,0:T(8,128)(4,1)S(1)} %iota_compare_fusion), kind=kOutput, calls=%fused_computation.32 | convolution fusion | flops 808452096 | bytes 1916928 | tf_op jit(solution)/shard_map/while/body/eval_jaxpr/hts,shp->thp/dot_general | solution.py:49
  33.7 9.1 %all-gather.7.cloned.1.call-done = bf16[128,128,64]{1,2,0:T(8,128)(2,1)} async-done(((bf16[16,128,64]{1,2,0:T(8,128)(2,1)}), bf16[128,128,64]{1,2,0:T(8,128)(2,1)}) %all-gather.7.cloned.1.call-update) | async-done | bytes 2097168 | tf_op jit(solution)/shard_map/all_gather | solution.py:18
  42.8 13.6 %while.37 = (s32[]{:T(128)}, f32[16,128,64]{2,1,0:T(8,128)S(1)}, s32[]{:T(128)}, bf16[8,16]{1,0:T(8,128)(2,1)S(1)}, bf16[8,16,128,64]{2,3,1,0:T(8,128)(2,1)}, /*index=5*/s32[]{:T(128)}, s32[]{:T(128)}) while((s32[]{:T(128)}, f32[16,128,64]{2,1,0:T(8,128)S(1)}, s32[]{:T(128)}, bf16[8,16]{1,0:T(8,128)(2,1)S(1)}, ...), condition=%wide.region_4.5_spmd.clone, body=%wide.region_3.4_spmd.clone.sunk | while | flops 655380 | bytes 2359569 | solution.py:35
  60.6 7.8 %psum.7 = f32[256]{0:T(256)S(1)} all-reduce(f32[256]{0:T(256)S(1)} %multiply_reduce_fusion), channel_id=1, replica_groups=mesh['seq'=8,'head'=4] {'head'}, use_global_device_ids=true, to_apply=%region_6.7 | all-reduce | flops 256 | bytes 2048 | tf_op jit(solution)/shard_map/psum | solution.py:173
  69.8 3.8 %collective-permute-start = (bf16[256,1024]{0,1:T(8,128)(2,1)S(1)}, bf16[256,1024]{0,1:T(8,128)(2,1)S(1)}, u32[]{:S(2)}, u32[]{:S(2)}) collective-permute-start(bf16[256,1024]{0,1:T(8,128)(2,1)S(1)} %copy.64), channel_id=1, source_target_pairs={{0,4},{4,8},{8,12},{12,16},{16,20},{20,24},{24,28},{28,0},{1,5},{5... | collective-permute-start | bytes 1572872 | tf_op jit(solution)/shard_map/ppermute | solution.py:134
  73.6 17.1 %collective-permute-done = bf16[256,1024]{0,1:T(8,128)(2,1)S(1)} collective-permute-done((bf16[256,1024]{0,1:T(8,128)(2,1)S(1)}, bf16[256,1024]{0,1:T(8,128)(2,1)S(1)}, u32[]{:S(2)}, u32[]{:S(2)}) %collective-permute-start) | collective-permute-done | bytes 524320 | tf_op jit(solution)/shard_map/ppermute | solution.py:134
  90.7 4.3 %collective-permute-start.2 = (bf16[256,1024]{0,1:T(8,128)(2,1)S(1)}, bf16[256,1024]{0,1:T(8,128)(2,1)}, u32[]{:S(2)}, u32[]{:S(2)}) collective-permute-start(bf16[256,1024]{0,1:T(8,128)(2,1)S(1)} %collective-permute-done), channel_id=1, source_target_pairs={{0,4},{4,8},{8,12},{12,16},{16,20},{20,24},{24,28},{28,0},{1,5},{5... | collective-permute-start | bytes 1572872 | tf_op jit(solution)/shard_map/ppermute | solution.py:134
  94.9 3.8 %collective-permute-done.1 = bf16[256,1024]{0,1:T(8,128)(2,1)S(1)} collective-permute-done((bf16[256,1024]{0,1:T(8,128)(2,1)S(1)}, bf16[256,1024]{0,1:T(8,128)(2,1)S(1)}, u32[]{:S(2)}, u32[]{:S(2)}) %collective-permute-start.1) | collective-permute-done | bytes 524320 | tf_op jit(solution)/shard_map/ppermute | solution.py:141
  98.8 18.9 %collective-permute-done.2 = bf16[256,1024]{0,1:T(8,128)(2,1)} collective-permute-done((bf16[256,1024]{0,1:T(8,128)(2,1)S(1)}, bf16[256,1024]{0,1:T(8,128)(2,1)}, u32[]{:S(2)}, u32[]{:S(2)}) %collective-permute-start.2) | collective-permute-done | bytes 524320 | tf_op jit(solution)/shard_map/ppermute | solution.py:134
  117.6 4.4 %collective-permute-start.4 = (bf16[256,1024]{0,1:T(8,128)(2,1)}, bf16[256,1024]{0,1:T(8,128)(2,1)S(1)}, u32[]{:S(2)}, u32[]{:S(2)}) collective-permute-start(bf16[256,1024]{0,1:T(8,128)(2,1)} %collective-permute-done.2), channel_id=1, source_target_pairs={{0,4},{4,8},{8,12},{12,16},{16,20},{20,24},{24,28},{28,0},{1,5},{5... | collective-permute-start | bytes 1572872 | tf_op jit(solution)/shard_map/ppermute | solution.py:134
  122.6 2.5 %broadcast_in_dim.94 = bf16[2048,1024]{0,1:T(8,128)(2,1)} broadcast(bf16[]{:T(256)} %constant.170.clone.1), dimensions={} | broadcast | bytes 4194306 | tf_op jit(solution)/shard_map/broadcast_in_dim | solution.py:124
  125.9 6.3 %collective-permute-start.5 = (bf16[256,1024]{0,1:T(8,128)(2,1)}, bf16[256,1024]{0,1:T(8,128)(2,1)S(1)}, u32[]{:S(2)}, u32[]{:S(2)}) collective-permute-start(bf16[256,1024]{0,1:T(8,128)(2,1)} %collective-permute-done.3), channel_id=1, source_target_pairs={{0,28},{4,0},{8,4},{12,8},{16,12},{20,16},{24,20},{28,24},{1,29},{... | collective-permute-start | bytes 1572872 | tf_op jit(solution)/shard_map/ppermute | solution.py:141
  133.1 4.0 %collective-permute-done.4 = bf16[256,1024]{0,1:T(8,128)(2,1)S(1)} collective-permute-done((bf16[256,1024]{0,1:T(8,128)(2,1)}, bf16[256,1024]{0,1:T(8,128)(2,1)S(1)}, u32[]{:S(2)}, u32[]{:S(2)}) %collective-permute-start.4) | collective-permute-done | bytes 524320 | tf_op jit(solution)/shard_map/ppermute | solution.py:134
  137.2 4.2 %collective-permute-start.6 = (bf16[256,1024]{0,1:T(8,128)(2,1)S(1)}, bf16[256,1024]{0,1:T(8,128)(2,1)S(1)}, u32[]{:S(2)}, u32[]{:S(2)}) collective-permute-start(bf16[256,1024]{0,1:T(8,128)(2,1)S(1)} %collective-permute-done.4), channel_id=1, source_target_pairs={{0,4},{4,8},{8,12},{12,16},{16,20},{20,24},{24,28},{28,0},{1,5},{5... | collective-permute-start | bytes 1572872 | tf_op jit(solution)/shard_map/ppermute | solution.py:134
  148.7 6.5 %copy.69 = bf16[2048,1024]{0,1:T(8,128)(2,1)} copy(bf16[2048,1024]{1,0:T(8,128)(2,1)} %all-gather.5.cloned.1.call-done) | data formatting | bytes 8388608 | tf_op jit(solution)/shard_map/while | solution.py:222
  155.3 29.1 %while.36 = (s32[]{:T(128)}, f32[8,256]{1,0:T(8,128)S(1)}, f32[8,256]{1,0:T(8,128)S(1)}, f32[8,256,128]{2,1,0:T(8,128)S(1)}, s32[256]{0:T(256)S(1)}, /*index=5*/...) while((s32[]{:T(128)}, f32[8,256]{1,0:T(8,128)S(1)}, ...), condition=%wide.region_12.13_spmd, body=%wide.region_7.12_spmd.sunk | while | flops 551162368 | bytes 22160688 | solution.py:222
  156.5 6.0 %conditional.2 = (f32[8,256]{1,0:T(8,128)S(1)}, f32[8,256]{1,0:T(8,128)S(1)}, f32[8,256,128]{2,1,0:T(8,128)S(1)}) conditional(s32[]{:T(128)} %convert_element_type.129, (s32[]{:T(128)}, s32[512]{0:T(512)S(1)}, s32[256]{0:T(256)S(1)}, bf16[2048,1024]{0,1:T(8,128)(2,1)}, bf16[256,8,128]{2,0,1:T(8,128)(2,1)S(1)}, /*index=5*/f32[8,256]{1,0:T(8,128)S(1)}, ...), branch_computations={%region_8.10_spmd, %region_11.11_spmd} | conditional | flops 551162368 | bytes 22142018 | solution.py:101
  160.4 2.1 %fusion.6 = f32[8,256,128]{2,1,0:T(8,128)S(1)} fusion(bf16[512,8,128]{0,2,1:T(8,128)(2,1)S(1)} %bitcast.91, f32[8,512,256]{2,1,0:T(8,128)S(1)} %get-tuple-element.477, f32[8,256]{1,0:T(8,128)S(1)} %max.5, pred[256,512]{0,1:T(8,128)(4,1)S(1)} %broadcast_compare_fusion, f32[8,256,128]{2,1,0:T(8,128)S(1)} %get-tuple-element.364, ...), kind=kOutput, calls=%fused_computation.7 | convolution fusion | flops 274202624 | bytes 7487488 | tf_op jit(solution)/shard_map/while/body/eval_jaxpr/cond/branch_0_fun/hqk,khd->hqd/dot_general | solution.py:94
  163.8 6.0 %conditional.2 = (f32[8,256]{1,0:T(8,128)S(1)}, f32[8,256]{1,0:T(8,128)S(1)}, f32[8,256,128]{2,1,0:T(8,128)S(1)}) conditional(s32[]{:T(128)} %convert_element_type.129, (s32[]{:T(128)}, s32[512]{0:T(512)S(1)}, s32[256]{0:T(256)S(1)}, bf16[2048,1024]{0,1:T(8,128)(2,1)}, bf16[256,8,128]{2,0,1:T(8,128)(2,1)S(1)}, /*index=5*/f32[8,256]{1,0:T(8,128)S(1)}, ...), branch_computations={%region_8.10_spmd, %region_11.11_spmd} | conditional | flops 551162368 | bytes 22142018 | solution.py:101
  167.7 2.1 %fusion.6 = f32[8,256,128]{2,1,0:T(8,128)S(1)} fusion(bf16[512,8,128]{0,2,1:T(8,128)(2,1)S(1)} %bitcast.91, f32[8,512,256]{2,1,0:T(8,128)S(1)} %get-tuple-element.477, f32[8,256]{1,0:T(8,128)S(1)} %max.5, pred[256,512]{0,1:T(8,128)(4,1)S(1)} %broadcast_compare_fusion, f32[8,256,128]{2,1,0:T(8,128)S(1)} %get-tuple-element.364, ...), kind=kOutput, calls=%fused_computation.7 | convolution fusion | flops 274202624 | bytes 7487488 | tf_op jit(solution)/shard_map/while/body/eval_jaxpr/cond/branch_0_fun/hqk,khd->hqd/dot_general | solution.py:94
  171.1 6.0 %conditional.2 = (f32[8,256]{1,0:T(8,128)S(1)}, f32[8,256]{1,0:T(8,128)S(1)}, f32[8,256,128]{2,1,0:T(8,128)S(1)}) conditional(s32[]{:T(128)} %convert_element_type.129, (s32[]{:T(128)}, s32[512]{0:T(512)S(1)}, s32[256]{0:T(256)S(1)}, bf16[2048,1024]{0,1:T(8,128)(2,1)}, bf16[256,8,128]{2,0,1:T(8,128)(2,1)S(1)}, /*index=5*/f32[8,256]{1,0:T(8,128)S(1)}, ...), branch_computations={%region_8.10_spmd, %region_11.11_spmd} | conditional | flops 551162368 | bytes 22142018 | solution.py:101
  178.4 6.0 %conditional.2 = (f32[8,256]{1,0:T(8,128)S(1)}, f32[8,256]{1,0:T(8,128)S(1)}, f32[8,256,128]{2,1,0:T(8,128)S(1)}) conditional(s32[]{:T(128)} %convert_element_type.129, (s32[]{:T(128)}, s32[512]{0:T(512)S(1)}, s32[256]{0:T(256)S(1)}, bf16[2048,1024]{0,1:T(8,128)(2,1)}, bf16[256,8,128]{2,0,1:T(8,128)(2,1)S(1)}, /*index=5*/f32[8,256]{1,0:T(8,128)S(1)}, ...), branch_computations={%region_8.10_spmd, %region_11.11_spmd} | conditional | flops 551162368 | bytes 22142018 | solution.py:101
  (141 shorter events, 58.6 us)
Async XLA Ops:
  7.2 21.9 %copy-start = (bf16[256,128]{1,0:T(8,128)(2,1)S(1)}, bf16[256,128]{1,0:T(8,128)(2,1)}, u32[]{:S(2)}) copy-start(bf16[256,128]{1,0:T(8,128)(2,1)} %param.19) | copy-start | bytes 196612
  7.2 35.6 %all-gather.7.cloned.1.call-start = ((), (), s32[]{:S(2)}) async-start(), calls=%async_computation.1 | async-start | bytes 2359296 | tf_op jit(solution)/shard_map/all_gather | solution.py:18
  13.4 135.3 %all-gather.5.cloned.1.call-start = ((), (), s32[]{:S(2)}) async-start(), calls=%async_computation | async-start | bytes 4718592 | tf_op jit(solution)/shard_map/all_gather | solution.py:190
  42.8 13.6 %copy-start.7 = (f32[16]{0:T(128)S(1)}, f32[16]{0:T(128)}, u32[]{:S(2)}) copy-start(f32[16]{0:T(128)} %param.22) | copy-start | bytes 196
  56.4 3.8 %copy-start.1 = (bf16[256,1024]{1,0:T(8,128)(2,1)S(1)}, bf16[256,1024]{1,0:T(8,128)(2,1)}, u32[]{:S(2)}) copy-start(bf16[256,1024]{1,0:T(8,128)(2,1)} %param.17) | copy-start | bytes 1572868
  56.4 11.9 %copy-start.6 = (f32[1024]{0:T(1024)S(1)}, f32[1024]{0:T(1024)}, u32[]{:S(2)}) copy-start(f32[1024]{0:T(1024)} %param.23) | copy-start | bytes 12292
  58.5 11.0 %copy-start.2 = (bf16[256,1024]{1,0:T(8,128)(2,1)S(1)}, bf16[256,1024]{1,0:T(8,128)(2,1)}, u32[]{:S(2)}) copy-start(bf16[256,1024]{1,0:T(8,128)(2,1)} %param.25) | copy-start | bytes 1572868
  58.5 63.5 %copy-start.3 = (bf16[256,1024]{1,0:T(8,128)(2,1)S(1)}, bf16[256,1024]{1,0:T(8,128)(2,1)}, u32[]{:S(2)}) copy-start(bf16[256,1024]{1,0:T(8,128)(2,1)} %param.24) | copy-start | bytes 1572868
  69.8 20.9 %collective-permute-start = (bf16[256,1024]{0,1:T(8,128)(2,1)S(1)}, bf16[256,1024]{0,1:T(8,128)(2,1)S(1)}, u32[]{:S(2)}, u32[]{:S(2)}) collective-permute-start(bf16[256,1024]{0,1:T(8,128)(2,1)S(1)} %copy.64), channel_id=1, source_target_pairs={{0,4},{4,8},{8,12},{12,16},{16,20},{20,24},{24,28},{28,0},{1,5},{5... | collective-permute-start | bytes 1572872 | tf_op jit(solution)/shard_map/ppermute | solution.py:134
  73.6 25.2 %collective-permute-start.1 = (bf16[256,1024]{0,1:T(8,128)(2,1)S(1)}, bf16[256,1024]{0,1:T(8,128)(2,1)S(1)}, u32[]{:S(2)}, u32[]{:S(2)}) collective-permute-start(bf16[256,1024]{0,1:T(8,128)(2,1)S(1)} %copy.64), channel_id=1, source_target_pairs={{0,28},{4,0},{8,4},{12,8},{16,12},{20,16},{24,20},{28,24},{1,29},{... | collective-permute-start | bytes 1572872 | tf_op jit(solution)/shard_map/ppermute | solution.py:141
  90.7 31.6 %copy-start.4 = (bf16[256,1024]{0,1:T(8,128)(2,1)}, bf16[256,1024]{0,1:T(8,128)(2,1)S(1)}, u32[]{:S(2)}) copy-start(bf16[256,1024]{0,1:T(8,128)(2,1)S(1)} %collective-permute-done) | copy-start | bytes 1572868
  90.7 27.0 %collective-permute-start.2 = (bf16[256,1024]{0,1:T(8,128)(2,1)S(1)}, bf16[256,1024]{0,1:T(8,128)(2,1)}, u32[]{:S(2)}, u32[]{:S(2)}) collective-permute-start(bf16[256,1024]{0,1:T(8,128)(2,1)S(1)} %collective-permute-done), channel_id=1, source_target_pairs={{0,4},{4,8},{8,12},{12,16},{16,20},{20,24},{24,28},{28,0},{1,5},{5... | collective-permute-start | bytes 1572872 | tf_op jit(solution)/shard_map/ppermute | solution.py:134
  98.8 27.2 %collective-permute-start.3 = (bf16[256,1024]{0,1:T(8,128)(2,1)S(1)}, bf16[256,1024]{0,1:T(8,128)(2,1)}, u32[]{:S(2)}, u32[]{:S(2)}) collective-permute-start(bf16[256,1024]{0,1:T(8,128)(2,1)S(1)} %collective-permute-done.1), channel_id=1, source_target_pairs={{0,28},{4,0},{8,4},{12,8},{16,12},{20,16},{24,20},{28,24},{1,29},{... | collective-permute-start | bytes 1572872 | tf_op jit(solution)/shard_map/ppermute | solution.py:141
  117.6 19.5 %collective-permute-start.4 = (bf16[256,1024]{0,1:T(8,128)(2,1)}, bf16[256,1024]{0,1:T(8,128)(2,1)S(1)}, u32[]{:S(2)}, u32[]{:S(2)}) collective-permute-start(bf16[256,1024]{0,1:T(8,128)(2,1)} %collective-permute-done.2), channel_id=1, source_target_pairs={{0,4},{4,8},{8,12},{12,16},{16,20},{20,24},{24,28},{28,0},{1,5},{5... | collective-permute-start | bytes 1572872 | tf_op jit(solution)/shard_map/ppermute | solution.py:134
  122.3 10.0 %copy-start.5 = (bf16[256,1024]{0,1:T(8,128)(2,1)S(1)}, bf16[256,1024]{0,1:T(8,128)(2,1)}, u32[]{:S(2)}) copy-start(bf16[256,1024]{0,1:T(8,128)(2,1)} %copy-done.4) | copy-start | bytes 1572868
  125.9 21.0 %collective-permute-start.5 = (bf16[256,1024]{0,1:T(8,128)(2,1)}, bf16[256,1024]{0,1:T(8,128)(2,1)S(1)}, u32[]{:S(2)}, u32[]{:S(2)}) collective-permute-start(bf16[256,1024]{0,1:T(8,128)(2,1)} %collective-permute-done.3), channel_id=1, source_target_pairs={{0,28},{4,0},{8,4},{12,8},{16,12},{20,16},{24,20},{28,24},{1,29},{... | collective-permute-start | bytes 1572872 | tf_op jit(solution)/shard_map/ppermute | solution.py:141
  137.2 10.7 %collective-permute-start.6 = (bf16[256,1024]{0,1:T(8,128)(2,1)S(1)}, bf16[256,1024]{0,1:T(8,128)(2,1)S(1)}, u32[]{:S(2)}, u32[]{:S(2)}) collective-permute-start(bf16[256,1024]{0,1:T(8,128)(2,1)S(1)} %collective-permute-done.4), channel_id=1, source_target_pairs={{0,4},{4,8},{8,12},{12,16},{16,20},{20,24},{24,28},{28,0},{1,5},{5... | collective-permute-start | bytes 1572872 | tf_op jit(solution)/shard_map/ppermute | solution.py:134
Sparse Core Ops, SparseCore 0:
  13.6 29.2 all-gather.6
  69.7 64.5 all-gather.4
